TPU v7x, 32 devices: a whole 2x2x4 slice. The times are simulated.
32 devices in a mesh: gx: 8 (over z, y), ha: 4 (over x, core).
Axes of the slice: x: 2, y: 2, z: 4, core: 2. Of those that a mesh axis runs over, the one named last changes fastest.
Arguments:
- value_field: float32 [8, 32, 16, 16], P('ha', None, 'gx'), may hold values from -6 to 6
- avoid_field: float32 [8, 32, 16, 16], P('ha', None, 'gx'), may hold values from -6 to 6
- sample_adjoint: float32 [8, 4, 8, 128], P('gx', 'ha'), may hold values from -6 to 6
- offset_y: float32 [8, 4, 8, 128], P('gx', 'ha'), may hold values from 0 to 1
- offset_s: float32 [8, 4, 8, 128], P('gx', 'ha'), may hold values from 0 to 1
- start_xy: int32 [8, 4, 8, 128], P('gx', 'ha'), may hold values from 0 to 30, as said below
- start_hs: int32 [8, 4, 8, 128], P('gx', 'ha'), may hold values from 0 to 62, as said below
- send_counts: int32 [8, 4, 8], P('gx', 'ha'), may hold values from 16 to 128, as said below
Outputs:
- next_value: float32 [8, 32, 16, 16], P('ha', None, 'gx')
- value_grad: float32 [8, 32, 16, 16], P('ha', None, 'gx')
- avoid_grad: float32 [8, 32, 16, 16], P('ha', None, 'gx')
Inputs may be any that keep to these rules, and one draw needn't show every extreme that they name: `start_xy`: the y cell of a start is at most 14. `start_hs`: the speed cell of a start is at most 30. `send_counts`: the live slots of a row are its first ones. For each index along ha, one owner drawn from the seed gets all 128 slots live from every sender.
All inputs are finite; a program needn't handle non-finite values.
Results may differ from a plain program's by a relative error of at most 0.00002.
Values sent between devices are 32-bit elements; how exact they have to be, the bound alone decides.
A program may use at most 64 MiB of HBM per device.

v0:
```python
import math
import jax
import jax.numpy as jnp
from jax import lax
from jax.sharding import PartitionSpec as P

TIME_STEP = 0.3
SHARPNESS = 2.0
SOFTENING = 0.1
TURN_RATE = 0.5
ACCELERATION = 0.3
SLOWEST = 0.2
SPEED_RANGE = 0.8
FASTEST = 1.0


def with_halo(block, sides, width):
    for axis, dim in sides:
        count = lax.axis_size(axis)
        forward = [(i, i + 1) for i in range(count - 1)]
        forward.append((count - 1, 0))
        backward = [(target, source) for source, target in forward]
        low = lax.ppermute(
            lax.slice_in_dim(block, block.shape[dim] - width, None, axis=dim), axis, forward
        )
        high = lax.ppermute(lax.slice_in_dim(block, 0, width, axis=dim), axis, backward)
        block = jnp.concatenate([low, block, high], axis=dim)
    return block


def smooth_abs(slope_value):
    return jnp.sqrt(slope_value * slope_value + SOFTENING * SOFTENING)


def edge_neighbours(grid_field, along_dim):
    length = grid_field.shape[along_dim]
    first_plane = lax.slice_in_dim(grid_field, 0, 1, axis=along_dim)
    last_plane = lax.slice_in_dim(grid_field, length - 1, length, axis=along_dim)
    upper_cells = jnp.concatenate(
        [lax.slice_in_dim(grid_field, 1, length, axis=along_dim), last_plane], along_dim
    )
    lower_cells = jnp.concatenate(
        [first_plane, lax.slice_in_dim(grid_field, 0, length - 1, axis=along_dim)], along_dim
    )
    return (upper_cells, lower_cells)


def linear_term(grid_field, upper_cells, lower_cells, factor):
    return (
        factor * (upper_cells - lower_cells) * 0.5
        - FASTEST * (upper_cells - 2.0 * grid_field + lower_cells) * 0.5
    )


def turn_term(grid_field, upper_cells, lower_cells, turn_rate):
    return turn_rate * smooth_abs(0.5 * (upper_cells - lower_cells)) - turn_rate * 0.5 * (
        upper_cells - 2.0 * grid_field + lower_cells
    )


def coefficients(head_index, total_heads, speeds):
    heading_angle = 2.0 * math.pi / total_heads * head_index.astype(jnp.float32)
    speed_cell = SLOWEST + SPEED_RANGE * jnp.arange(speeds, dtype=jnp.int32).astype(jnp.float32) / (
        speeds - 1
    )
    along_x = jnp.cos(heading_angle)[:, None, None, None] * speed_cell[None, :, None, None]
    along_y = jnp.sin(heading_angle)[:, None, None, None] * speed_cell[None, :, None, None]
    return (along_x, along_y)


def to_columns(grid_field):
    return jnp.swapaxes(
        lax.all_to_all(grid_field, "gx", split_axis=3, concat_axis=2, tiled=True), 2, 3
    )


def from_columns(grid_field):
    return lax.all_to_all(
        jnp.swapaxes(grid_field, 2, 3), "gx", split_axis=2, concat_axis=3, tiled=True
    )


def corner_weights(weight, offset_rows, offset_speed):
    return [
        weight * (1.0 - offset_rows) * (1.0 - offset_speed),
        weight * offset_rows * (1.0 - offset_speed),
        weight * (1.0 - offset_rows) * offset_speed,
        weight * offset_rows * offset_speed,
    ]


def on_device(
    value_field, avoid_field, sample_adjoint, offset_y, offset_s, start_xy, start_hs, send_counts
):
    head_count, speeds, row_count, line_count = value_field.shape
    groups = lax.axis_size("gx")
    slot_count = sample_adjoint.shape[3]
    head_index = lax.axis_index("ha") * head_count + jnp.arange(head_count, dtype=jnp.int32)
    along_x, along_y = coefficients(head_index, head_count * lax.axis_size("ha"), speeds)
    padded = with_halo(value_field, (("ha", 0),), 1)
    ahead_plane = padded[2:]
    behind = padded[:-2]
    slope_turn = 0.5 * (ahead_plane - behind)
    turning = TURN_RATE * smooth_abs(slope_turn) - TURN_RATE * 0.5 * (
        ahead_plane - 2.0 * value_field + behind
    )

    def local_terms(grid_field):
        upper_cells, lower_cells = edge_neighbours(grid_field, 3)
        summed = linear_term(grid_field, upper_cells, lower_cells, along_y)
        upper_cells, lower_cells = edge_neighbours(grid_field, 1)
        return summed + turn_term(grid_field, upper_cells, lower_cells, ACCELERATION)

    local_part, local_back = jax.vjp(local_terms, value_field)

    def line_term(grid_field):
        upper_cells, lower_cells = edge_neighbours(grid_field, 3)
        return linear_term(grid_field, upper_cells, lower_cells, along_x)

    across, line_back = jax.vjp(line_term, to_columns(value_field))
    across = from_columns(across)
    hamilton = across + local_part + turning
    relaxed = value_field - TIME_STEP * hamilton
    excess = SHARPNESS * (relaxed - avoid_field)
    next_value = avoid_field + jax.nn.softplus(excess) / SHARPNESS
    blend_share = jax.nn.sigmoid(excess)
    counts = send_counts.reshape(groups)
    live_slot = jnp.arange(slot_count, dtype=jnp.int32)[None, :] < counts[:, None]
    weight = jnp.where(live_slot, sample_adjoint.reshape(groups, slot_count), 0.0)
    offset_rows = offset_y.reshape(groups, slot_count)
    offset_speed = offset_s.reshape(groups, slot_count)
    cell_rows = start_xy.reshape(groups, slot_count)
    states = start_hs.reshape(groups, slot_count)
    payload = jnp.concatenate(corner_weights(weight, offset_rows, offset_speed), axis=1)
    payload, cell_rows, states = (
        lax.all_to_all(payload, "gx", split_axis=0, concat_axis=0, tiled=True),
        lax.all_to_all(cell_rows, "gx", split_axis=0, concat_axis=0, tiled=True),
        lax.all_to_all(states, "gx", split_axis=0, concat_axis=0, tiled=True),
    )
    pieces = jnp.split(payload, 4, axis=1)
    plane = row_count * line_count
    flat_index = states * plane + cell_rows
    cell_index = jnp.concatenate(
        [flat_index, flat_index + 1, flat_index + plane, flat_index + plane + 1], axis=0
    )
    deposit_sum = jnp.zeros((head_count * speeds * plane,), jnp.float32)
    deposit_sum = deposit_sum.at[cell_index.reshape(-1)].add(
        jnp.concatenate(pieces, axis=0).reshape(-1)
    )
    adjoint = deposit_sum.reshape(value_field.shape)
    avoid_grad = adjoint * (1.0 - blend_share)
    carried = adjoint * blend_share
    pull_turn = carried * TURN_RATE * slope_turn / smooth_abs(slope_turn)
    stacked = with_halo(jnp.stack([carried, pull_turn]), (("ha", 1),), 1)
    back_turn = 0.5 * (stacked[1, :-2] - stacked[1, 2:]) - TURN_RATE * 0.5 * (
        stacked[0, 2:] - 2.0 * carried + stacked[0, :-2]
    )
    back_local = local_back(carried)[0]
    back_across = from_columns(line_back(to_columns(carried))[0])
    value_grad = carried - TIME_STEP * (back_across + back_local + back_turn)
    return (next_value, value_grad, avoid_grad)


def solution(mesh):
    in_specs = (
        P("ha", None, "gx", None),
        P("ha", None, "gx", None),
        P("gx", "ha", None, None),
        P("gx", "ha", None, None),
        P("gx", "ha", None, None),
        P("gx", "ha", None, None),
        P("gx", "ha", None, None),
        P("gx", "ha", None),
    )
    out_specs = (P("ha", None, "gx", None), P("ha", None, "gx", None), P("ha", None, "gx", None))
    return jax.shard_map(
        on_device, mesh=mesh, in_specs=in_specs, out_specs=out_specs, check_vma=False
    )
```

profile of v0, /device:TPU:0, one launch (start us, length us, event | category | flops | bytes accessed | tf_op | source)
XLA Modules:
  0.0 99.8 jit_solution(10327407511817762513)
XLA Ops:
  0.6 7.3 %all-to-all-start.2 = ((s32[8,1,128]{2,1,0:T(1,128)}), s32[8,1,128]{2,1,0:T(1,128)S(1)}, u32[]{:S(2)}, u32[]{:S(2)}) async-start(s32[8,1,128]{2,1,0:T(1,128)} %bitcast.167), calls=%async_computation.2 | async-start | bytes 8192 | tf_op jit(solution)/shard_map/all_to_all | solution.py:138
  7.9 0.8 fusion.40
  8.7 0.7 collective-permute-start
  10.5 3.9 %all-to-all-done.2 = s32[8,1,128]{2,1,0:T(1,128)S(1)} async-done(((s32[8,1,128]{2,1,0:T(1,128)}), s32[8,1,128]{2,1,0:T(1,128)S(1)}, u32[]{:S(2)}, u32[]{:S(2)}) %all-to-all-start.2) | async-done | bytes 4128 | tf_op jit(solution)/shard_map/all_to_all | solution.py:138
  14.3 3.3 %all-to-all-start.3 = ((s32[8,1,128]{2,1,0:T(1,128)}), s32[8,1,128]{2,1,0:T(1,128)S(1)}, u32[]{:S(2)}, u32[]{:S(2)}) async-start(s32[8,1,128]{2,1,0:T(1,128)} %bitcast.11), calls=%async_computation.3 | async-start | bytes 8192 | tf_op jit(solution)/shard_map/all_to_all | solution.py:137
  17.7 0.6 all_to_all.84
  18.3 0.7 reshape.163
  19.0 5.0 %all-to-all-done.3 = s32[8,1,128]{2,1,0:T(1,128)S(1)} async-done(((s32[8,1,128]{2,1,0:T(1,128)}), s32[8,1,128]{2,1,0:T(1,128)S(1)}, u32[]{:S(2)}, u32[]{:S(2)}) %all-to-all-start.3) | async-done | bytes 4128 | tf_op jit(solution)/shard_map/all_to_all | solution.py:137
  24.0 3.3 %all-to-all-start = ((f32[8,1,256]{2,1,0:T(1,128)}), f32[8,1,256]{2,1,0:T(1,128)S(1)}, u32[]{:S(2)}, u32[]{:S(2)}) async-start(f32[8,1,256]{2,1,0:T(1,128)} %reshape.163), calls=%async_computation | async-start | bytes 16384 | tf_op jit(solution)/shard_map/all_to_all | solution.py:73
  27.4 6.4 %all-to-all-done = f32[8,1,256]{2,1,0:T(1,128)S(1)} async-done(((f32[8,1,256]{2,1,0:T(1,128)}), f32[8,1,256]{2,1,0:T(1,128)S(1)}, u32[]{:S(2)}, u32[]{:S(2)}) %all-to-all-start) | async-done | bytes 8224 | tf_op jit(solution)/shard_map/all_to_all | solution.py:73
  33.8 3.3 %all-to-all-start.4 = ((f32[8,1,512]{2,1,0:T(1,128)}), f32[8,1,512]{2,1,0:T(1,128)S(1)}, u32[]{:S(2)}, u32[]{:S(2)}) async-start(f32[8,1,512]{2,1,0:T(1,128)} %all_to_all.84), calls=%async_computation.4 | async-start | bytes 32768 | tf_op jit(solution)/shard_map/all_to_all | solution.py:136
  37.7 0.7 reduce
  38.6 0.7 reshape.165
  39.3 4.3 %all-to-all-done.4 = f32[8,1,512]{2,1,0:T(1,128)S(1)} async-done(((f32[8,1,512]{2,1,0:T(1,128)}), f32[8,1,512]{2,1,0:T(1,128)S(1)}, u32[]{:S(2)}, u32[]{:S(2)}) %all-to-all-start.4) | async-done | bytes 16416 | tf_op jit(solution)/shard_map/all_to_all | solution.py:136
  43.6 3.3 %all-to-all-start.1 = ((f32[8,1,256]{2,1,0:T(1,128)}), f32[8,1,256]{2,1,0:T(1,128)S(1)}, u32[]{:S(2)}, u32[]{:S(2)}) async-start(f32[8,1,256]{2,1,0:T(1,128)} %reshape.165), calls=%async_computation.1 | async-start | bytes 16384 | tf_op jit(solution)/shard_map/all_to_all | solution.py:78
  47.0 22.0 %scatter_custom_fusion = f32[2048]{0:T(1024)S(1)} fusion(s32[4096]{0:T(1024)S(1)} %bitcast.166, f32[4096]{0:T(1024)S(1)} %maximum_bitcast_fusion, f32[]{:T(128)} %constant.18.clone.1), kind=kCustom, calls=%fused_computation.78 | custom fusion | flops 4096 | bytes 8196 | tf_op jit(solution)/shard_map/scatter-add | solution.py:147
  69.2 0.7 reduce.1
  70.1 0.7 copy-done.1
  70.8 0.8 subtract_multiply_fusion
  71.6 0.7 negate_add_fusion.1
  72.3 0.7 reshape.167
  73.0 6.0 %all-to-all-start.5 = ((f32[8,1,256]{2,1,0:T(1,128)}), f32[8,1,256]{2,1,0:T(1,128)S(1)}, u32[]{:S(2)}, u32[]{:S(2)}) async-start(f32[8,1,256]{2,1,0:T(1,128)} %reshape.167), calls=%async_computation.5 | async-start | bytes 16384 | tf_op jit(solution)/shard_map/all_to_all | solution.py:73
  79.0 6.5 %all-to-all-done.5 = f32[8,1,256]{2,1,0:T(1,128)S(1)} async-done(((f32[8,1,256]{2,1,0:T(1,128)}), f32[8,1,256]{2,1,0:T(1,128)S(1)}, u32[]{:S(2)}, u32[]{:S(2)}) %all-to-all-start.5) | async-done | bytes 8224 | tf_op jit(solution)/shard_map/all_to_all | solution.py:73
  85.4 0.7 reduce.2
  86.3 0.6 copy-done.5
  87.1 0.7 reshape.169
  87.8 3.3 %all-to-all-start.6 = ((f32[8,1,256]{2,1,0:T(1,128)}), f32[8,1,256]{2,1,0:T(1,128)S(1)}, u32[]{:S(2)}, u32[]{:S(2)}) async-start(f32[8,1,256]{2,1,0:T(1,128)} %reshape.169), calls=%async_computation.6 | async-start | bytes 16384 | tf_op jit(solution)/shard_map/all_to_all | solution.py:78
  91.2 1.7 %collective-permute-start.3 = (f32[2,1,32,2,16]{2,4,3,1,0:T(8,128)S(1)}, f32[2,1,32,2,16]{2,4,3,1,0:T(8,128)S(1)}, u32[]{:S(2)}, u32[]{:S(2)}) collective-permute-start(f32[2,1,32,2,16]{2,4,3,1,0:T(8,128)S(1)} %get-tuple-element.11), channel_id=1, source_target_pairs={{1,0},{2,1},{3,2},{0,3},{5,4},{6,5},{7,6},{4,7},{9,8},{10,9},{11,1... | collective-permute-start | bytes 24584 | tf_op jit(solution)/shard_map/ppermute | solution.py:26
  93.1 4.5 %all-to-all-done.6 = f32[8,1,256]{2,1,0:T(1,128)S(1)} async-done(((f32[8,1,256]{2,1,0:T(1,128)}), f32[8,1,256]{2,1,0:T(1,128)S(1)}, u32[]{:S(2)}, u32[]{:S(2)}) %all-to-all-start.6) | async-done | bytes 8224 | tf_op jit(solution)/shard_map/all_to_all | solution.py:78
  97.6 0.7 reduce.3
  98.5 0.6 copy-done.7
  99.1 0.7 fusion.9
  (67 shorter events, 2.8 us)
Async XLA Ops:
  0.6 13.7 %all-to-all-start.2 = ((s32[8,1,128]{2,1,0:T(1,128)}), s32[8,1,128]{2,1,0:T(1,128)S(1)}, u32[]{:S(2)}, u32[]{:S(2)}) async-start(s32[8,1,128]{2,1,0:T(1,128)} %bitcast.167), calls=%async_computation.2 | async-start | bytes 8192 | tf_op jit(solution)/shard_map/all_to_all | solution.py:138
  7.9 1.5 %copy-start = (f32[2,32,2,16]{1,3,2,0:T(8,128)S(1)}, f32[2,32,2,16]{1,3,2,0:T(8,128)}, u32[]{:S(2)}) copy-start(f32[2,32,2,16]{1,3,2,0:T(8,128)} %param.8) | copy-start | bytes 24580
  8.7 61.4 %collective-permute-start = (f32[1,32,2,16]{1,3,2,0:T(8,128)S(1)}, f32[1,32,2,16]{1,3,2,0:T(8,128)S(1)}, u32[]{:S(2)}, u32[]{:S(2)}) collective-permute-start(f32[1,32,2,16]{1,3,2,0:T(8,128)S(1)} %get-tuple-element.34), channel_id=1, source_target_pairs={{1,0},{2,1},{3,2},{0,3},{5,4},{6,5},{7,6},{4,7},{9,8},{10,9},{11,1... | collective-permute-start | bytes 12296 | tf_op jit(solution)/shard_map/ppermute | solution.py:26
  9.4 60.7 %collective-permute-start.1 = (f32[1,32,2,16]{1,3,2,0:T(8,128)S(1)}, f32[1,32,2,16]{1,3,2,0:T(8,128)S(1)}, u32[]{:S(2)}, u32[]{:S(2)}) collective-permute-start(f32[1,32,2,16]{1,3,2,0:T(8,128)S(1)} %get-tuple-element.35), channel_id=1, source_target_pairs={{0,1},{1,2},{2,3},{3,0},{4,5},{5,6},{6,7},{7,4},{8,9},{9,10},{10,1... | collective-permute-start | bytes 12296 | tf_op jit(solution)/shard_map/ppermute | solution.py:23
  9.5 0.7 copy-start.4
  9.6 0.7 copy-start.3
  9.6 0.7 copy-start.2
  9.6 0.7 copy-start.6
  14.3 9.6 %all-to-all-start.3 = ((s32[8,1,128]{2,1,0:T(1,128)}), s32[8,1,128]{2,1,0:T(1,128)S(1)}, u32[]{:S(2)}, u32[]{:S(2)}) async-start(s32[8,1,128]{2,1,0:T(1,128)} %bitcast.11), calls=%async_computation.3 | async-start | bytes 8192 | tf_op jit(solution)/shard_map/all_to_all | solution.py:137
  24.0 9.8 %all-to-all-start = ((f32[8,1,256]{2,1,0:T(1,128)}), f32[8,1,256]{2,1,0:T(1,128)S(1)}, u32[]{:S(2)}, u32[]{:S(2)}) async-start(f32[8,1,256]{2,1,0:T(1,128)} %reshape.163), calls=%async_computation | async-start | bytes 16384 | tf_op jit(solution)/shard_map/all_to_all | solution.py:73
  33.8 9.9 %all-to-all-start.4 = ((f32[8,1,512]{2,1,0:T(1,128)}), f32[8,1,512]{2,1,0:T(1,128)S(1)}, u32[]{:S(2)}, u32[]{:S(2)}) async-start(f32[8,1,512]{2,1,0:T(1,128)} %all_to_all.84), calls=%async_computation.4 | async-start | bytes 32768 | tf_op jit(solution)/shard_map/all_to_all | solution.py:136
  43.6 25.6 %all-to-all-start.1 = ((f32[8,1,256]{2,1,0:T(1,128)}), f32[8,1,256]{2,1,0:T(1,128)S(1)}, u32[]{:S(2)}, u32[]{:S(2)}) async-start(f32[8,1,256]{2,1,0:T(1,128)} %reshape.165), calls=%async_computation.1 | async-start | bytes 16384 | tf_op jit(solution)/shard_map/all_to_all | solution.py:78
  70.1 0.8 copy-start.1
  73.0 12.5 %all-to-all-start.5 = ((f32[8,1,256]{2,1,0:T(1,128)}), f32[8,1,256]{2,1,0:T(1,128)S(1)}, u32[]{:S(2)}, u32[]{:S(2)}) async-start(f32[8,1,256]{2,1,0:T(1,128)} %reshape.167), calls=%async_computation.5 | async-start | bytes 16384 | tf_op jit(solution)/shard_map/all_to_all | solution.py:73
  86.3 0.7 copy-start.5
  87.8 9.8 %all-to-all-start.6 = ((f32[8,1,256]{2,1,0:T(1,128)}), f32[8,1,256]{2,1,0:T(1,128)S(1)}, u32[]{:S(2)}, u32[]{:S(2)}) async-start(f32[8,1,256]{2,1,0:T(1,128)} %reshape.169), calls=%async_computation.6 | async-start | bytes 16384 | tf_op jit(solution)/shard_map/all_to_all | solution.py:78
  91.1 7.3 %collective-permute-start.2 = (f32[2,1,32,2,16]{2,4,3,1,0:T(8,128)S(1)}, f32[2,1,32,2,16]{2,4,3,1,0:T(8,128)S(1)}, u32[]{:S(2)}, u32[]{:S(2)}) collective-permute-start(f32[2,1,32,2,16]{2,4,3,1,0:T(8,128)S(1)} %get-tuple-element.12), channel_id=1, source_target_pairs={{0,1},{1,2},{2,3},{3,0},{4,5},{5,6},{6,7},{7,4},{8,9},{9,10},{10,1... | collective-permute-start | bytes 24584 | tf_op jit(solution)/shard_map/ppermute | solution.py:23
  91.2 7.2 %collective-permute-start.3 = (f32[2,1,32,2,16]{2,4,3,1,0:T(8,128)S(1)}, f32[2,1,32,2,16]{2,4,3,1,0:T(8,128)S(1)}, u32[]{:S(2)}, u32[]{:S(2)}) collective-permute-start(f32[2,1,32,2,16]{2,4,3,1,0:T(8,128)S(1)} %get-tuple-element.11), channel_id=1, source_target_pairs={{1,0},{2,1},{3,2},{0,3},{5,4},{6,5},{7,6},{4,7},{9,8},{10,9},{11,1... | collective-permute-start | bytes 24584 | tf_op jit(solution)/shard_map/ppermute | solution.py:26
  98.5 0.7 copy-start.7
where the time goes:
time: 101 us; the launch traced here: 99.8 us
  starting transfers between devices  32.4 us (32%)
  waiting for transfers between devices  30.5 us (30%)
  other arithmetic  27.4 us (27%)
  local copies, waits for them, and re-layouts  8.55 us (8%)
  between operations  1.07 us (1%)
    scatter-add x1, other arithmetic, on_device(): deposit_sum.at[cell_index.reshape(-1)]  22 us
    all_to_all x2, waiting for transfers between devices, to_columns(): lax.all_to_all(grid_field, 'gx', split_axis=3, concat_axis=2, tiled=True)  12.9 us
    all_to_all x2, starting transfers between devices, to_columns(): lax.all_to_all(grid_field, 'gx', split_axis=3, concat_axis=2, tiled=True)  9.31 us
    all_to_all x1, starting transfers between devices, on_device(): lax.all_to_all(states, 'gx', split_axis=0, concat_axis=0, tiled=True)  7.29 us
    all_to_all x2, starting transfers between devices, from_columns(): lax.all_to_all(jnp.swapaxes(grid_field, 2, 3), 'gx', split_axis=2, concat...  6.67 us
    unnamed x26, local copies, waits for them, and re-layouts  5.85 us
    all_to_all x1, waiting for transfers between devices, on_device(): lax.all_to_all(cell_rows, 'gx', split_axis=0, concat_axis=0, tiled=True)  4.97 us
    all_to_all x2, waiting for transfers between devices, from_columns(): lax.all_to_all(jnp.swapaxes(grid_field, 2, 3), 'gx', split_axis=2, concat...  4.47 us
  transfers between devices with their start and end apart: 11, of which 6 were waited for; matrix products, arithmetic and copies ran while one was open for 28% of the time, Pallas kernels for 0%

commit v1 on v0

--- a/solution.py
+++ b/solution.py
@@ -70,7 +70,14 @@
 
 def to_columns(grid_field):
     return jnp.swapaxes(
-        lax.all_to_all(grid_field, "gx", split_axis=3, concat_axis=2, tiled=True), 2, 3
+        jnp.concatenate(
+            lax.all_to_all(
+                jnp.stack(jnp.split(grid_field, lax.psum(1, "gx"), axis=3), axis=0), "gx", 0, 0
+            ),
+            axis=2,
+        ),
+        2,
+        3,
     )
 
 

time: 101 us -> 101 us (level)
    unnamed x26 -> x39, local copies, waits for them, and re-layouts: 5.85 us -> 5.97 us
where the time goes in v1:
time: 101 us; the launch traced here: 99.9 us
  starting transfers between devices  32.4 us (32%)
  waiting for transfers between devices  30.4 us (30%)
  other arithmetic  27.4 us (27%)
  local copies, waits for them, and re-layouts  8.68 us (9%)
  between operations  1.12 us (1%)
    scatter-add x1, other arithmetic, on_device(): deposit_sum.at[cell_index.reshape(-1)]  22 us
    all_to_all x2, waiting for transfers between devices, to_columns(): lax.all_to_all(jnp.stack(jnp.split(grid_field, lax.psum(1, 'gx'), axis=3)...  12.9 us
    all_to_all x2, starting transfers between devices, to_columns(): lax.all_to_all(jnp.stack(jnp.split(grid_field, lax.psum(1, 'gx'), axis=3)...  9.31 us
    all_to_all x1, starting transfers between devices, on_device(): lax.all_to_all(states, 'gx', split_axis=0, concat_axis=0, tiled=True)  7.29 us
    all_to_all x2, starting transfers between devices, from_columns(): lax.all_to_all(jnp.swapaxes(grid_field, 2, 3), 'gx', split_axis=2, concat...  6.67 us
    unnamed x39, local copies, waits for them, and re-layouts  5.97 us
    all_to_all x1, waiting for transfers between devices, on_device(): lax.all_to_all(cell_rows, 'gx', split_axis=0, concat_axis=0, tiled=True)  4.99 us
    all_to_all x2, waiting for transfers between devices, from_columns(): lax.all_to_all(jnp.swapaxes(grid_field, 2, 3), 'gx', split_axis=2, concat...  4.47 us
  transfers between devices with their start and end apart: 11, of which 6 were waited for; matrix products, arithmetic and copies ran while one was open for 28% of the time, Pallas kernels for 0%

profile of v1, /device:TPU:0, one launch (start us, length us, event | category | flops | bytes accessed | tf_op | source)
XLA Modules:
  0.0 99.9 jit_solution(9006966550618875637)
XLA Ops:
  0.6 7.3 %all-to-all-start.2 = ((s32[8,1,128]{2,1,0:T(1,128)}), s32[8,1,128]{2,1,0:T(1,128)S(1)}, u32[]{:S(2)}, u32[]{:S(2)}) async-start(s32[8,1,128]{2,1,0:T(1,128)} %bitcast.208), calls=%async_computation.2 | async-start | bytes 8192 | tf_op jit(solution)/shard_map/all_to_all | solution.py:145
  7.9 0.8 fusion.40
  8.7 0.7 collective-permute-start
  10.6 3.7 %all-to-all-done.2 = s32[8,1,128]{2,1,0:T(1,128)S(1)} async-done(((s32[8,1,128]{2,1,0:T(1,128)}), s32[8,1,128]{2,1,0:T(1,128)S(1)}, u32[]{:S(2)}, u32[]{:S(2)}) %all-to-all-start.2) | async-done | bytes 4128 | tf_op jit(solution)/shard_map/all_to_all | solution.py:145
  14.3 3.3 %all-to-all-start.3 = ((s32[8,1,128]{2,1,0:T(1,128)}), s32[8,1,128]{2,1,0:T(1,128)S(1)}, u32[]{:S(2)}, u32[]{:S(2)}) async-start(s32[8,1,128]{2,1,0:T(1,128)} %bitcast.17), calls=%async_computation.3 | async-start | bytes 8192 | tf_op jit(solution)/shard_map/all_to_all | solution.py:144
  17.6 0.6 all_to_all.61
  18.3 0.7 reshape.179
  19.0 5.0 %all-to-all-done.3 = s32[8,1,128]{2,1,0:T(1,128)S(1)} async-done(((s32[8,1,128]{2,1,0:T(1,128)}), s32[8,1,128]{2,1,0:T(1,128)S(1)}, u32[]{:S(2)}, u32[]{:S(2)}) %all-to-all-start.3) | async-done | bytes 4128 | tf_op jit(solution)/shard_map/all_to_all | solution.py:144
  24.0 3.3 %all-to-all-start = ((f32[8,1,256]{2,1,0:T(1,128)}), f32[8,1,256]{2,1,0:T(1,128)S(1)}, u32[]{:S(2)}, u32[]{:S(2)}) async-start(f32[8,1,256]{2,1,0:T(1,128)} %reshape.179), calls=%async_computation | async-start | bytes 16384 | tf_op jit(solution)/shard_map/all_to_all | solution.py:74
  27.4 6.4 %all-to-all-done = f32[8,1,256]{2,1,0:T(1,128)S(1)} async-done(((f32[8,1,256]{2,1,0:T(1,128)}), f32[8,1,256]{2,1,0:T(1,128)S(1)}, u32[]{:S(2)}, u32[]{:S(2)}) %all-to-all-start) | async-done | bytes 8224 | tf_op jit(solution)/shard_map/all_to_all | solution.py:74
  33.8 3.3 %all-to-all-start.4 = ((f32[8,1,512]{2,1,0:T(1,128)}), f32[8,1,512]{2,1,0:T(1,128)S(1)}, u32[]{:S(2)}, u32[]{:S(2)}) async-start(f32[8,1,512]{2,1,0:T(1,128)} %all_to_all.61), calls=%async_computation.4 | async-start | bytes 32768 | tf_op jit(solution)/shard_map/all_to_all | solution.py:143
  37.7 0.7 reduce
  38.6 0.7 reshape.181
  39.3 4.3 %all-to-all-done.4 = f32[8,1,512]{2,1,0:T(1,128)S(1)} async-done(((f32[8,1,512]{2,1,0:T(1,128)}), f32[8,1,512]{2,1,0:T(1,128)S(1)}, u32[]{:S(2)}, u32[]{:S(2)}) %all-to-all-start.4) | async-done | bytes 16416 | tf_op jit(solution)/shard_map/all_to_all | solution.py:143
  43.6 3.3 %all-to-all-start.1 = ((f32[8,1,256]{2,1,0:T(1,128)}), f32[8,1,256]{2,1,0:T(1,128)S(1)}, u32[]{:S(2)}, u32[]{:S(2)}) async-start(f32[8,1,256]{2,1,0:T(1,128)} %reshape.181), calls=%async_computation.1 | async-start | bytes 16384 | tf_op jit(solution)/shard_map/all_to_all | solution.py:85
  47.0 22.0 %scatter_custom_fusion = f32[2048]{0:T(1024)S(1)} fusion(s32[4096]{0:T(1024)S(1)} %bitcast.207, f32[4096]{0:T(1024)S(1)} %maximum_bitcast_fusion, f32[]{:T(128)} %constant.18.clone.1), kind=kCustom, calls=%fused_computation.102 | custom fusion | flops 4096 | bytes 8196 | tf_op jit(solution)/shard_map/scatter-add | solution.py:154
  69.2 0.7 reduce.1
  70.1 0.7 copy-done.1
  70.8 0.8 subtract_multiply_fusion
  71.6 0.7 negate_add_fusion.1
  72.3 0.7 reshape.183
  73.0 6.0 %all-to-all-start.5 = ((f32[8,1,256]{2,1,0:T(1,128)}), f32[8,1,256]{2,1,0:T(1,128)S(1)}, u32[]{:S(2)}, u32[]{:S(2)}) async-start(f32[8,1,256]{2,1,0:T(1,128)} %reshape.183), calls=%async_computation.5 | async-start | bytes 16384 | tf_op jit(solution)/shard_map/all_to_all | solution.py:74
  79.0 6.5 %all-to-all-done.5 = f32[8,1,256]{2,1,0:T(1,128)S(1)} async-done(((f32[8,1,256]{2,1,0:T(1,128)}), f32[8,1,256]{2,1,0:T(1,128)S(1)}, u32[]{:S(2)}, u32[]{:S(2)}) %all-to-all-start.5) | async-done | bytes 8224 | tf_op jit(solution)/shard_map/all_to_all | solution.py:74
  85.5 0.7 reduce.2
  86.4 0.6 copy-done.5
  87.2 0.7 reshape.185
  87.9 3.3 %all-to-all-start.6 = ((f32[8,1,256]{2,1,0:T(1,128)}), f32[8,1,256]{2,1,0:T(1,128)S(1)}, u32[]{:S(2)}, u32[]{:S(2)}) async-start(f32[8,1,256]{2,1,0:T(1,128)} %reshape.185), calls=%async_computation.6 | async-start | bytes 16384 | tf_op jit(solution)/shard_map/all_to_all | solution.py:85
  91.3 1.7 %collective-permute-start.3 = (f32[2,1,32,2,16]{2,4,3,1,0:T(8,128)S(1)}, f32[2,1,32,2,16]{2,4,3,1,0:T(8,128)S(1)}, u32[]{:S(2)}, u32[]{:S(2)}) collective-permute-start(f32[2,1,32,2,16]{2,4,3,1,0:T(8,128)S(1)} %get-tuple-element.11), channel_id=1, source_target_pairs={{1,0},{2,1},{3,2},{0,3},{5,4},{6,5},{7,6},{4,7},{9,8},{10,9},{11,1... | collective-permute-start | bytes 24584 | tf_op jit(solution)/shard_map/ppermute | solution.py:26
  93.2 4.5 %all-to-all-done.6 = f32[8,1,256]{2,1,0:T(1,128)S(1)} async-done(((f32[8,1,256]{2,1,0:T(1,128)}), f32[8,1,256]{2,1,0:T(1,128)S(1)}, u32[]{:S(2)}, u32[]{:S(2)}) %all-to-all-start.6) | async-done | bytes 8224 | tf_op jit(solution)/shard_map/all_to_all | solution.py:85
  97.7 0.7 reduce.3
  98.5 0.6 copy-done.7
  99.2 0.7 fusion.9
  (82 shorter events, 3.0 us)
Async XLA Ops:
  0.6 13.7 %all-to-all-start.2 = ((s32[8,1,128]{2,1,0:T(1,128)}), s32[8,1,128]{2,1,0:T(1,128)S(1)}, u32[]{:S(2)}, u32[]{:S(2)}) async-start(s32[8,1,128]{2,1,0:T(1,128)} %bitcast.208), calls=%async_computation.2 | async-start | bytes 8192 | tf_op jit(solution)/shard_map/all_to_all | solution.py:145
  7.9 1.5 %copy-start = (f32[2,32,2,16]{1,3,2,0:T(8,128)S(1)}, f32[2,32,2,16]{1,3,2,0:T(8,128)}, u32[]{:S(2)}) copy-start(f32[2,32,2,16]{1,3,2,0:T(8,128)} %param.8) | copy-start | bytes 24580
  8.7 61.4 %collective-permute-start = (f32[1,32,2,16]{1,3,2,0:T(8,128)S(1)}, f32[1,32,2,16]{1,3,2,0:T(8,128)S(1)}, u32[]{:S(2)}, u32[]{:S(2)}) collective-permute-start(f32[1,32,2,16]{1,3,2,0:T(8,128)S(1)} %get-tuple-element.34), channel_id=1, source_target_pairs={{1,0},{2,1},{3,2},{0,3},{5,4},{6,5},{7,6},{4,7},{9,8},{10,9},{11,1... | collective-permute-start | bytes 12296 | tf_op jit(solution)/shard_map/ppermute | solution.py:26
  9.4 60.7 %collective-permute-start.1 = (f32[1,32,2,16]{1,3,2,0:T(8,128)S(1)}, f32[1,32,2,16]{1,3,2,0:T(8,128)S(1)}, u32[]{:S(2)}, u32[]{:S(2)}) collective-permute-start(f32[1,32,2,16]{1,3,2,0:T(8,128)S(1)} %get-tuple-element.35), channel_id=1, source_target_pairs={{0,1},{1,2},{2,3},{3,0},{4,5},{5,6},{6,7},{7,4},{8,9},{9,10},{10,1... | collective-permute-start | bytes 12296 | tf_op jit(solution)/shard_map/ppermute | solution.py:23
  9.7 0.7 copy-start.4
  9.7 0.7 copy-start.3
  9.7 0.7 copy-start.2
  9.8 0.7 copy-start.6
  14.3 9.6 %all-to-all-start.3 = ((s32[8,1,128]{2,1,0:T(1,128)}), s32[8,1,128]{2,1,0:T(1,128)S(1)}, u32[]{:S(2)}, u32[]{:S(2)}) async-start(s32[8,1,128]{2,1,0:T(1,128)} %bitcast.17), calls=%async_computation.3 | async-start | bytes 8192 | tf_op jit(solution)/shard_map/all_to_all | solution.py:144
  24.0 9.8 %all-to-all-start = ((f32[8,1,256]{2,1,0:T(1,128)}), f32[8,1,256]{2,1,0:T(1,128)S(1)}, u32[]{:S(2)}, u32[]{:S(2)}) async-start(f32[8,1,256]{2,1,0:T(1,128)} %reshape.179), calls=%async_computation | async-start | bytes 16384 | tf_op jit(solution)/shard_map/all_to_all | solution.py:74
  33.8 9.9 %all-to-all-start.4 = ((f32[8,1,512]{2,1,0:T(1,128)}), f32[8,1,512]{2,1,0:T(1,128)S(1)}, u32[]{:S(2)}, u32[]{:S(2)}) async-start(f32[8,1,512]{2,1,0:T(1,128)} %all_to_all.61), calls=%async_computation.4 | async-start | bytes 32768 | tf_op jit(solution)/shard_map/all_to_all | solution.py:143
  43.6 25.6 %all-to-all-start.1 = ((f32[8,1,256]{2,1,0:T(1,128)}), f32[8,1,256]{2,1,0:T(1,128)S(1)}, u32[]{:S(2)}, u32[]{:S(2)}) async-start(f32[8,1,256]{2,1,0:T(1,128)} %reshape.181), calls=%async_computation.1 | async-start | bytes 16384 | tf_op jit(solution)/shard_map/all_to_all | solution.py:85
  70.1 0.8 copy-start.1
  73.0 12.5 %all-to-all-start.5 = ((f32[8,1,256]{2,1,0:T(1,128)}), f32[8,1,256]{2,1,0:T(1,128)S(1)}, u32[]{:S(2)}, u32[]{:S(2)}) async-start(f32[8,1,256]{2,1,0:T(1,128)} %reshape.183), calls=%async_computation.5 | async-start | bytes 16384 | tf_op jit(solution)/shard_map/all_to_all | solution.py:74
  86.4 0.7 copy-start.5
  87.9 9.8 %all-to-all-start.6 = ((f32[8,1,256]{2,1,0:T(1,128)}), f32[8,1,256]{2,1,0:T(1,128)S(1)}, u32[]{:S(2)}, u32[]{:S(2)}) async-start(f32[8,1,256]{2,1,0:T(1,128)} %reshape.185), calls=%async_computation.6 | async-start | bytes 16384 | tf_op jit(solution)/shard_map/all_to_all | solution.py:85
  91.2 7.3 %collective-permute-start.2 = (f32[2,1,32,2,16]{2,4,3,1,0:T(8,128)S(1)}, f32[2,1,32,2,16]{2,4,3,1,0:T(8,128)S(1)}, u32[]{:S(2)}, u32[]{:S(2)}) collective-permute-start(f32[2,1,32,2,16]{2,4,3,1,0:T(8,128)S(1)} %get-tuple-element.12), channel_id=1, source_target_pairs={{0,1},{1,2},{2,3},{3,0},{4,5},{5,6},{6,7},{7,4},{8,9},{9,10},{10,1... | collective-permute-start | bytes 24584 | tf_op jit(solution)/shard_map/ppermute | solution.py:23
  91.3 7.2 %collective-permute-start.3 = (f32[2,1,32,2,16]{2,4,3,1,0:T(8,128)S(1)}, f32[2,1,32,2,16]{2,4,3,1,0:T(8,128)S(1)}, u32[]{:S(2)}, u32[]{:S(2)}) collective-permute-start(f32[2,1,32,2,16]{2,4,3,1,0:T(8,128)S(1)} %get-tuple-element.11), channel_id=1, source_target_pairs={{1,0},{2,1},{3,2},{0,3},{5,4},{6,5},{7,6},{4,7},{9,8},{10,9},{11,1... | collective-permute-start | bytes 24584 | tf_op jit(solution)/shard_map/ppermute | solution.py:26
  98.5 0.7 copy-start.7
